TPU v7x, 32 devices: a whole 2x2x4 slice. The times are simulated.
32 devices in a mesh: cfg: 2 (over core), tm: 2 (over x), space: 8 (over z, y).
Axes of the slice: x: 2, y: 2, z: 4, core: 2. Of those that a mesh axis runs over, the one named last changes fastest.
Arguments:
- solutions: bfloat16 [4, 2, 3, 1024, 384], P(('cfg', 'tm'), None, None, 'space'), parts along dimension 0, may hold values from -6 to 6
- eigvecs: bfloat16 [4, 2, 3, 1024, 384], P(('cfg', 'tm'), None, None, 'space'), parts along dimension 0, may hold values from -0.078125 to 0.078125
- meson: bfloat16 [4, 4, 2, 384, 384], P(None, ('cfg', 'tm')), parts along dimension 1, may hold values from -0.015625 to 0.015625
- momenta: int32 [4, 3], replicated, may hold values from -3 to 3
- source_time: int32 [384], replicated, may hold values from 0 to 1
- dilution: int32 [384], replicated, may hold values from 0 to 3
Outputs:
- blocks: float32 [4, 2, 384, 4, 384], P(None, None, ('tm', 'space'), 'cfg'), parts along dimension 3
There are 2 independent parts, one for each index of `cfg`. A program takes and returns all parts, laid end to end along the dimension named above; an argument that names none is the same for every part. Nothing has to cross between parts.
All inputs are finite; a program needn't handle non-finite values.
Results may differ from a plain program's by a relative error of at most 0.0056.
Values may be sent and summed in bfloat16 or wider, within the bound.
A program may use at most 64 MiB of HBM per device.

v0:
```python
import jax
import jax.numpy as jnp
from jax import lax
from jax.sharding import PartitionSpec as P

SIDE = 48
NDIL = 4


def contract(first_op, second_op):
    return lax.dot_general(
        first_op, second_op, (((1,), (1,)), ((0,), (0,))), preferred_element_type=jnp.float32
    )


def regroup(array, time_count, space_count, cols_local):
    leading = array.shape[:-1]
    split = array.reshape(leading + (time_count, space_count, cols_local))
    return jnp.swapaxes(split, -3, -2).reshape(leading + (time_count * space_count * cols_local,))


def ungroup(array, time_count, space_count, cols_local):
    leading = array.shape[:-1]
    split = array.reshape(leading + (space_count, time_count, cols_local))
    return jnp.swapaxes(split, -3, -2).reshape(leading + (time_count * space_count * cols_local,))


def project(stack_real, stack_imag, vec_real, vec_imag, set_count, amount):
    real_part = contract(stack_real, vec_real) + contract(stack_imag, vec_imag)
    imag_part = contract(stack_imag, vec_real) - contract(stack_real, vec_imag)
    stacked = jnp.stack([real_part, imag_part], 2)
    times_local = stacked.shape[0]
    stacked = stacked.reshape(times_local, amount, set_count, 2, stacked.shape[-1])
    return jnp.transpose(stacked, (1, 0, 2, 3, 4))


def momentum_blocks(momentum, meson):
    coef_real = momentum[:, :, :, 0]
    coef_imag = momentum[:, :, :, 1]
    meson_real = meson[:, :, 0]
    meson_imag = meson[:, :, 1]
    left_real = jnp.einsum(
        "atpk,ptkl->ptal", coef_real, meson_real, preferred_element_type=jnp.float32
    ) + jnp.einsum("atpk,ptkl->ptal", coef_imag, meson_imag, preferred_element_type=jnp.float32)
    left_imag = jnp.einsum(
        "atpk,ptkl->ptal", coef_real, meson_imag, preferred_element_type=jnp.float32
    ) - jnp.einsum("atpk,ptkl->ptal", coef_imag, meson_real, preferred_element_type=jnp.float32)
    return (left_real.astype(jnp.bfloat16), left_imag.astype(jnp.bfloat16))


def meson_block(portion, patterns_all, left_real, left_imag):
    vectors = portion.shape[-1]
    dilution_mask = (
        (jnp.arange(vectors, dtype=jnp.int32) % NDIL)[None, :] == patterns_all[:, None]
    ).astype(jnp.bfloat16)
    zero_mom = portion * dilution_mask[:, None, None, :]
    zero_real = zero_mom[:, :, 0]
    zero_imag = zero_mom[:, :, 1]
    real_part = jnp.einsum(
        "ptal,btl->tapb", left_real, zero_real, preferred_element_type=jnp.float32
    ) - jnp.einsum("ptal,btl->tapb", left_imag, zero_imag, preferred_element_type=jnp.float32)
    imag_part = jnp.einsum(
        "ptal,btl->tapb", left_real, zero_imag, preferred_element_type=jnp.float32
    ) + jnp.einsum("ptal,btl->tapb", left_imag, zero_real, preferred_element_type=jnp.float32)
    return jnp.stack([real_part, imag_part], 3)


def body(solutions, eigvecs, meson, momenta, source_time, dilution):
    times_local, _, colors, sites_local, columns = solutions.shape
    vectors = eigvecs.shape[4]
    moments = momenta.shape[0]
    space_count = lax.axis_size("space")
    time_count = lax.axis_size("tm")
    rows_local = columns // space_count
    cols_local = columns // (space_count * time_count)
    times_total = times_local * time_count
    grouped = regroup(solutions, time_count, space_count, cols_local)
    patterns_all = regroup(dilution, time_count, space_count, cols_local)
    site_index = lax.axis_index("space") * sites_local + jnp.arange(sites_local, dtype=jnp.int32)
    coordinates = jnp.stack(
        [site_index % SIDE, site_index // SIDE % SIDE, site_index // (SIDE * SIDE)], 0
    )
    windings = jnp.sum(momenta[:, :, None] * coordinates[None], 1)
    angles = 2.0 * jnp.pi / SIDE * windings.astype(jnp.float32)
    cosine = jnp.cos(angles)[:, None, None, :, None]
    sine_part = jnp.sin(angles)[:, None, None, :, None]
    solve_real = grouped[:, 0].astype(jnp.float32)
    solve_imag = grouped[:, 1].astype(jnp.float32)
    phased_real = cosine * solve_real[None] + sine_part * solve_imag[None]
    phased_imag = cosine * solve_imag[None] - sine_part * solve_real[None]
    flat_rows = colors * sites_local
    phased_real = (
        jnp.moveaxis(phased_real, 0, -1)
        .reshape(times_local, flat_rows, columns * moments)
        .astype(jnp.bfloat16)
    )
    phased_imag = (
        jnp.moveaxis(phased_imag, 0, -1)
        .reshape(times_local, flat_rows, columns * moments)
        .astype(jnp.bfloat16)
    )
    base_real = grouped[:, 0].reshape(times_local, flat_rows, columns)
    base_imag = grouped[:, 1].reshape(times_local, flat_rows, columns)
    vec_real = eigvecs[:, 0].reshape(times_local, flat_rows, vectors)
    vec_imag = eigvecs[:, 1].reshape(times_local, flat_rows, vectors)
    zero_terms = project(base_real, base_imag, vec_real, vec_imag, 1, columns)
    zero_all = lax.psum(zero_terms, "space").astype(jnp.bfloat16)[:, :, 0]
    momentum = lax.psum_scatter(
        project(
            phased_real,
            phased_imag,
            vec_real,
            vec_imag,
            moments,
            rows_local * lax.axis_size("space"),
        ),
        "space",
        scatter_dimension=0,
        tiled=True,
    ).astype(jnp.bfloat16)
    left_real, left_imag = momentum_blocks(momentum, meson)
    blocks = meson_block(zero_all, patterns_all, left_real, left_imag)
    outgoing = blocks.reshape(times_local, time_count, cols_local, moments, 2, columns)
    first_row = (lax.axis_index("tm") * space_count + lax.axis_index("space")) * cols_local
    my_sources = lax.dynamic_slice_in_dim(source_time, first_row, cols_local)
    offsets = (
        my_sources[:, None] + jnp.arange(times_total, dtype=jnp.int32)[None, :]
    ) % times_total
    selector = (
        offsets[:, :, None] == jnp.arange(times_total, dtype=jnp.int32)[None, None, :]
    ).astype(jnp.float32)
    received = lax.all_to_all(
        outgoing.astype(jnp.bfloat16), "tm", split_axis=1, concat_axis=0, tiled=True
    ).astype(outgoing.dtype)
    by_time = received.reshape(times_total, cols_local, received.shape[3], 2, columns)
    by_time = ungroup(by_time, time_count, space_count, cols_local)
    return jnp.einsum("adt,taprb->pradb", selector, by_time, precision=lax.Precision.HIGHEST)


def solution(mesh):
    return jax.shard_map(
        body,
        mesh=mesh,
        in_specs=(
            P(("cfg", "tm"), None, None, "space", None),
            P(("cfg", "tm"), None, None, "space", None),
            P(None, ("cfg", "tm"), None, None, None),
            P(),
            P(),
            P(),
        ),
        out_specs=P(None, None, ("tm", "space"), "cfg", None),
        check_vma=False,
    )
```

profile of v0, /device:TPU:0, one launch (start us, length us, event | category | flops | bytes accessed | tf_op | source)
XLA Modules:
  0.0 181.8 jit_solution(11664704982364159849)
XLA Ops:
  6.6 0.8 copy.53
  7.5 1.4 copy.50
  10.1 1.7 add_convert_fusion
  11.8 0.9 fusion.8
  12.6 2.3 %fusion.4 = f32[1536,384]{1,0:T(8,128)} fusion(bf16[384,384]{1,0:T(8,128)(2,1)S(1)} %bitcast.165, bf16[192,8,3,128]{3,2,1,0:T(4,128)(2,1)S(1)} %bitcast.154), kind=kOutput, calls=%fused_computation.15 | convolution fusion | flops 452984832 | bytes 3833856 | tf_op jit(solution)/shard_map/dot_general | solution.py:11
  14.9 2.3 %convolution_add_fusion = f32[1536,384]{1,0:T(8,128)} fusion(f32[1536,384]{1,0:T(8,128)S(1)} %fusion.8, bf16[384,384]{1,0:T(8,128)(2,1)S(1)} %bitcast.162, bf16[192,8,3,128]{3,2,1,0:T(4,128)(2,1)S(1)} %bitcast.155), kind=kOutput, calls=%fused_computation.4 | convolution fusion | flops 453574656 | bytes 6193152 | tf_op jit(solution)/shard_map/dot_general | solution.py:11
  17.3 3.6 %stack.37 = f32[384,1,4,1,384]{4,2,0,3,1:T(4,128)} reshape(f32[1536,384]{1,0:T(8,128)} %convolution_add_fusion) | data formatting | bytes 4718592 | tf_op jit(solution)/shard_map/stack | solution.py:31
  20.9 3.4 %copy.56 = f32[384,1,4,1,384]{4,0,2,3,1:T(8,128)} copy(f32[384,1,4,1,384]{4,2,0,3,1:T(4,128)} %stack.37) | data formatting | bytes 4718592 | tf_op jit(solution)/shard_map/stack | solution.py:31
  24.2 2.3 %convolution_subtract_fusion = f32[1536,384]{1,0:T(8,128)} fusion(f32[1536,384]{1,0:T(8,128)S(1)} %copy-done, bf16[384,384]{1,0:T(8,128)(2,1)S(1)} %bitcast.163, bf16[192,8,3,128]{3,2,1,0:T(4,128)(2,1)S(1)} %bitcast.153), kind=kOutput, calls=%fused_computation.3 | convolution fusion | flops 453574656 | bytes 6193152 | tf_op jit(solution)/shard_map/dot_general | solution.py:11
  26.6 2.6 %stack.38 = f32[384,1,4,1,384]{4,2,0,3,1:T(4,128)S(1)} reshape(f32[1536,384]{1,0:T(8,128)} %convolution_subtract_fusion) | data formatting | bytes 4718592 | tf_op jit(solution)/shard_map/stack | solution.py:31
  29.4 1.5 copy-done.2
  30.9 2.4 %pad_maximum_fusion = f32[384,1,4,2,384]{4,0,2,3,1:T(8,128)} fusion(f32[384,1,4,1,384]{4,0,2,3,1:T(8,128)S(1)} %copy.57, f32[384,1,4,1,384]{4,0,2,3,1:T(8,128)S(1)} %copy-done.2), kind=kLoop, calls=%fused_computation | loop fusion | flops 1179648 | bytes 9437184 | tf_op jit(solution)/shard_map/stack | solution.py:31
  35.2 0.9 dynamic_slice.3
  36.1 0.9 compare_convert_fusion
  37.0 92.2 %all-reduce.1 = bf16[384,1,1,2,384]{4,0,3,2,1:T(8,128)(2,1)} all-reduce(f32[384,1,1,2,384]{4,0,3,2,1:T(8,128)S(1)} %maximum_bitcast_fusion), channel_id=1, replica_groups=mesh['cfg'=2,'tm'=2,'space'=8] {'space'}, use_global_device_ids=true, to_apply=%region_0.1 | all-reduce | flops 294912 | bytes 1769472 | tf_op jit(solution)/shard_map/psum | solution.py:107
  129.2 1.2 bitcast_multiply_fusion
  130.4 25.2 %reduce-scatter.2.cloned.1.call-done = f32[48,1,4,2,384]{4,0,2,3,1:T(8,128)} async-done(((f32[384,1,4,2,384]{4,0,2,3,1:T(8,128)}), f32[48,1,4,2,384]{4,0,2,3,1:T(8,128)}) %reduce-scatter.2.cloned.1.call-update) | async-done | bytes 589840 | tf_op jit(solution)/shard_map/reduce_scatter | solution.py:108
  155.6 1.1 convert_element_type.87
  159.0 0.7 copy.65
  159.8 3.6 %all-to-all-start = ((bf16[1,2,24,4,2,384]{5,2,3,4,0,1:T(8,128)(2,1)}), bf16[1,2,24,4,2,384]{5,2,3,4,0,1:T(8,128)(2,1)S(1)}, u32[]{:S(2)}, u32[]{:S(2)}) async-start(bf16[1,2,24,4,2,384]{5,2,3,4,0,1:T(8,128)(2,1)} %copy.65), calls=%async_computation.1 | async-start | bytes 589824 | tf_op jit(solution)/shard_map/all_to_all | solution.py:132
  163.5 5.2 %all-to-all-done = bf16[1,2,24,4,2,384]{5,2,3,4,0,1:T(8,128)(2,1)S(1)} async-done(((bf16[1,2,24,4,2,384]{5,2,3,4,0,1:T(8,128)(2,1)}), bf16[1,2,24,4,2,384]{5,2,3,4,0,1:T(8,128)(2,1)S(1)}, u32[]{:S(2)}, u32[]{:S(2)}) %all-to-all-start) | async-done | bytes 294944 | tf_op jit(solution)/shard_map/all_to_all | solution.py:132
  168.7 2.0 %reshape_reshape.3 = bf16[2,24,4,2,8,2,24]{6,5,4,1,2,3,0:T(2,128)(2,1)S(1)} reshape(bf16[1,2,24,4,2,384]{5,2,3,4,0,1:T(8,128)(2,1)S(1)} %all-to-all-done) | data formatting | bytes 589824 | tf_op jit(solution)/shard_map/reshape;reshape | solution.py:24
  171.2 2.2 %reshape.428 = bf16[2,24,4,2,384]{4,0,3,2,1:T(2,128)(2,1)S(1)} reshape(bf16[2,24,4,2,2,8,24]{6,5,4,0,3,2,1:T(8,128)(2,1)S(1)} %bitcast.161) | data formatting | bytes 589824 | tf_op jit(solution)/shard_map/reshape | solution.py:25
  173.9 1.0 copy.63
  (47 shorter events, 6.6 us)
Async XLA Ops:
  6.5 149.1 %reduce-scatter.2.cloned.1.call-start = ((), (), s32[]{:S(2)}) async-start(), calls=%async_computation.2 | async-start | bytes 5308416 | tf_op jit(solution)/shard_map/reduce_scatter | solution.py:108
  8.9 1.1 copy-start.3
  10.1 4.9 %copy-start.4 = (bf16[1,1,3,128,384]{4,3,2,1,0:T(8,128)(2,1)}, bf16[1,1,3,128,384]{4,3,2,1,0:T(8,128)(2,1)S(1)}, u32[]{:S(2)}) copy-start(bf16[1,1,3,128,384]{4,3,2,1,0:T(8,128)(2,1)S(1)} %get-tuple-element.7) | copy-start | bytes 884740
  20.8 3.4 %copy-start = (f32[1536,384]{1,0:T(8,128)S(1)}, f32[1536,384]{1,0:T(8,128)}, u32[]{:S(2)}) copy-start(f32[1536,384]{1,0:T(8,128)} %fusion.4) | copy-start | bytes 7077892
  20.9 3.4 %copy-start.5 = (bf16[1,1,3,128,384]{4,3,2,1,0:T(8,128)(2,1)S(1)}, bf16[1,1,3,128,384]{4,3,2,1,0:T(8,128)(2,1)}, u32[]{:S(2)}) copy-start(bf16[1,1,3,128,384]{4,3,2,1,0:T(8,128)(2,1)} %copy-done.4) | copy-start | bytes 884740
  29.2 1.7 copy-start.2
  34.3 0.7 copy-start.6
  35.0 121.7 %copy-start.1 = (bf16[4,1,2,384,384]{4,3,2,1,0:T(8,128)(2,1)S(1)}, bf16[4,1,2,384,384]{4,3,2,1,0:T(8,128)(2,1)}, u32[]{:S(2)}) copy-start(bf16[4,1,2,384,384]{4,3,2,1,0:T(8,128)(2,1)} %param.8) | copy-start | bytes 7077892
  159.8 9.0 %all-to-all-start = ((bf16[1,2,24,4,2,384]{5,2,3,4,0,1:T(8,128)(2,1)}), bf16[1,2,24,4,2,384]{5,2,3,4,0,1:T(8,128)(2,1)S(1)}, u32[]{:S(2)}, u32[]{:S(2)}) async-start(bf16[1,2,24,4,2,384]{5,2,3,4,0,1:T(8,128)(2,1)} %copy.65), calls=%async_computation.1 | async-start | bytes 589824 | tf_op jit(solution)/shard_map/all_to_all | solution.py:132
Sparse Core Ops, SparseCore 0:
  33.4 122.1 reduce-scatter.1
where the time goes:
time: 182 us
  blocking collectives  92.2 us (51%)
  waiting for transfers between devices  30.5 us (17%)
  local copies, waits for them, and re-layouts  22.2 us (12%)
  between operations  13.7 us (8%)
  matrix products  11.9 us (7%)
  other arithmetic  7.73 us (4%)
  starting transfers between devices  3.63 us (2%)
    psum x1, blocking collectives, body(): zero_all = lax.psum(zero_terms, 'space').astype(jnp.bfloat16)[:, :, 0]  92.2 us
    reduce_scatter x1, waiting for transfers between devices, body(): lax.psum_scatter(project(phased_real, phased_imag, vec_real, vec_imag, mo...  25.2 us
    another operation x4, local copies, waits for them, and re-layouts, project(): stacked = jnp.stack([real_part, imag_part], 2)  9.73 us
    dot_general x8, matrix products, contract(): lax.dot_general(first_op, second_op, (((1,), (1,)), ((0,), (0,))), prefer...  9.17 us
    all_to_all x1, waiting for transfers between devices, body(): lax.all_to_all(outgoing.astype(jnp.bfloat16), 'tm', split_axis=1, concat_...  5.24 us
    unnamed x16, local copies, waits for them, and re-layouts  4.05 us
  transfers between devices with their start and end apart: 2, of which 2 were waited for; matrix products, arithmetic and copies ran while one was open for 3% of the time, Pallas kernels for 0%

commit v1 on v0

--- a/solution.py
+++ b/solution.py
@@ -104,7 +104,7 @@
     vec_real = eigvecs[:, 0].reshape(times_local, flat_rows, vectors)
     vec_imag = eigvecs[:, 1].reshape(times_local, flat_rows, vectors)
     zero_terms = project(base_real, base_imag, vec_real, vec_imag, 1, columns)
-    zero_all = lax.psum(zero_terms, "space").astype(jnp.bfloat16)[:, :, 0]
+    zero_all = jnp.sum(lax.all_gather(zero_terms, "space"), axis=0).astype(jnp.bfloat16)[:, :, 0]
     momentum = lax.psum_scatter(
         project(
             phased_real,

time: 182 us -> 300 us (1.65)
  waiting for transfers between devices: 30.5 us -> 237 us
  blocking collectives: 92.2 us -> 0 us
  other arithmetic: 7.73 us -> 11.1 us
    all_gather x0 -> x1, waiting for transfers between devices: none -> 137 us  [body(): lax.all_gather(zero_terms, 'space')]
    psum x1 -> x0, blocking collectives: 92.2 us -> none  [body(): zero_all = lax.psum(zero_terms, 'space').astype(jnp.bfloat16)[:, :, 0]]
    reduce_scatter x1, waiting for transfers between devices: 25.2 us -> 94.9 us  [body(): lax.psum_scatter(project(phased_real, phased_imag, vec_real, vec_imag, mo...]
    reduce_sum x0 -> x1, other arithmetic: none -> 4.19 us  [body(): jnp.sum(lax.all_gather(zero_terms, 'space'), axis=0).astype(jnp.bfloat16)]
  transfers between devices with their start and end apart: 2 -> 3, of which waited for: 2 -> 3; matrix products, arithmetic and copies ran while one was open for 3% -> 2% of each run, Pallas kernels for 0% -> 0%
where the time goes in v1:
time: 300 us; the launch traced here: 299 us
  waiting for transfers between devices  237 us (79%)
  local copies, waits for them, and re-layouts  21.8 us (7%)
  between operations  13.7 us (5%)
  matrix products  11.9 us (4%)
  other arithmetic  11.1 us (4%)
  starting transfers between devices  3.67 us (1%)
    all_gather x1, waiting for transfers between devices, body(): lax.all_gather(zero_terms, 'space')  137 us
    reduce_scatter x1, waiting for transfers between devices, body(): lax.psum_scatter(project(phased_real, phased_imag, vec_real, vec_imag, mo...  94.9 us
    another operation x4, local copies, waits for them, and re-layouts, project(): stacked = jnp.stack([real_part, imag_part], 2)  9.7 us
    dot_general x8, matrix products, contract(): lax.dot_general(first_op, second_op, (((1,), (1,)), ((0,), (0,))), prefer...  9.14 us
  transfers between devices with their start and end apart: 3, of which 3 were waited for; matrix products, arithmetic and copies ran while one was open for 2% of the time, Pallas kernels for 0%

profile of v1, /device:TPU:0, one launch (start us, length us, event | category | flops | bytes accessed | tf_op | source)
XLA Modules:
  0.0 299.0 jit_solution(3352481038959387750)
XLA Ops:
  6.6 0.8 copy.53
  7.5 1.4 copy.50
  10.1 1.7 add_convert_fusion
  11.8 0.9 fusion.8
  12.6 2.3 fusion.4
  14.9 2.3 convolution_add_fusion
  17.2 3.6 %stack.37 = f32[384,1,4,1,384]{4,2,0,3,1:T(4,128)} reshape(f32[1536,384]{1,0:T(8,128)} %convolution_add_fusion) | data formatting | bytes 4718592 | tf_op jit(solution)/shard_map/stack | solution.py:31
  20.8 3.4 %copy.56 = f32[384,1,4,1,384]{4,0,2,3,1:T(8,128)} copy(f32[384,1,4,1,384]{4,2,0,3,1:T(4,128)} %stack.37) | data formatting | bytes 4718592 | tf_op jit(solution)/shard_map/stack | solution.py:31
  24.2 2.3 convolution_subtract_fusion
  26.5 2.6 stack.38
  29.3 1.5 copy-done.2
  30.8 2.5 pad_maximum_fusion
  34.8 1.1 pad_maximum_fusion.1
  36.1 0.8 dynamic_slice.3
  37.0 94.9 %reduce-scatter.2.cloned.1.call-done = f32[48,1,4,2,384]{4,0,2,3,1:T(8,128)} async-done(((f32[384,1,4,2,384]{4,0,2,3,1:T(8,128)}), f32[48,1,4,2,384]{4,0,2,3,1:T(8,128)}) %reduce-scatter.2.cloned.1.call-update) | async-done | bytes 589840 | tf_op jit(solution)/shard_map/reduce_scatter | solution.py:108
  131.9 1.1 convert_element_type.101
  134.2 136.8 %all-gather.3.cloned.1.call-done = f32[8,384,2,384]{3,1,2,0:T(8,128)} async-done(((f32[1,384,2,384]{3,1,2,0:T(8,128)}), f32[8,384,2,384]{3,1,2,0:T(8,128)}) %all-gather.3.cloned.1.call-update) | async-done | bytes 9437200 | tf_op jit(solution)/shard_map/all_gather | solution.py:107
  271.0 4.2 %reduce.1 = bf16[384,2,384]{2,0,1:T(8,128)(2,1)S(1)} reduce(f32[8,384,2,384]{3,1,2,0:T(8,128)} %all-gather.3.cloned.1.call-done, f32[]{:T(128)} %constant.62.clone.1), dimensions={0}, to_apply=%region_0.1 | reduce | flops 2064384 | bytes 10027012 | tf_op jit(solution)/shard_map/reduce_sum | solution.py:107
  276.4 0.7 copy.65
  277.1 3.6 %all-to-all-start = ((bf16[1,2,24,4,2,384]{5,2,3,4,0,1:T(8,128)(2,1)}), bf16[1,2,24,4,2,384]{5,2,3,4,0,1:T(8,128)(2,1)S(1)}, u32[]{:S(2)}, u32[]{:S(2)}) async-start(bf16[1,2,24,4,2,384]{5,2,3,4,0,1:T(8,128)(2,1)} %copy.65), calls=%async_computation.1 | async-start | bytes 589824 | tf_op jit(solution)/shard_map/all_to_all | solution.py:132
  280.9 5.1 %all-to-all-done = bf16[1,2,24,4,2,384]{5,2,3,4,0,1:T(8,128)(2,1)S(1)} async-done(((bf16[1,2,24,4,2,384]{5,2,3,4,0,1:T(8,128)(2,1)}), bf16[1,2,24,4,2,384]{5,2,3,4,0,1:T(8,128)(2,1)S(1)}, u32[]{:S(2)}, u32[]{:S(2)}) %all-to-all-start) | async-done | bytes 294944 | tf_op jit(solution)/shard_map/all_to_all | solution.py:132
  285.9 2.0 reshape_reshape.3
  288.4 2.2 reshape.434
  291.1 1.0 copy.63
  (50 shorter events, 6.6 us)
Async XLA Ops:
  6.5 125.4 %reduce-scatter.2.cloned.1.call-start = ((), (), s32[]{:S(2)}) async-start(), calls=%async_computation.2 | async-start | bytes 5308416 | tf_op jit(solution)/shard_map/reduce_scatter | solution.py:108
  8.9 1.1 copy-start.3
  10.1 4.9 %copy-start.4 = (bf16[1,1,3,128,384]{4,3,2,1,0:T(8,128)(2,1)}, bf16[1,1,3,128,384]{4,3,2,1,0:T(8,128)(2,1)S(1)}, u32[]{:S(2)}) copy-start(bf16[1,1,3,128,384]{4,3,2,1,0:T(8,128)(2,1)S(1)} %get-tuple-element.7) | copy-start | bytes 884740
  20.8 3.4 %copy-start = (f32[1536,384]{1,0:T(8,128)S(1)}, f32[1536,384]{1,0:T(8,128)}, u32[]{:S(2)}) copy-start(f32[1536,384]{1,0:T(8,128)} %fusion.4) | copy-start | bytes 7077892
  20.8 3.4 %copy-start.5 = (bf16[1,1,3,128,384]{4,3,2,1,0:T(8,128)(2,1)S(1)}, bf16[1,1,3,128,384]{4,3,2,1,0:T(8,128)(2,1)}, u32[]{:S(2)}) copy-start(bf16[1,1,3,128,384]{4,3,2,1,0:T(8,128)(2,1)} %copy-done.4) | copy-start | bytes 884740
  29.1 1.7 copy-start.2
  33.3 237.7 %all-gather.3.cloned.1.call-start = ((), (), s32[]{:S(2)}) async-start(), calls=%async_computation.3 | async-start | bytes 10616832 | tf_op jit(solution)/shard_map/all_gather | solution.py:107
  34.4 1.5 copy-start.6
  34.8 98.2 %copy-start.1 = (bf16[4,1,2,384,384]{4,3,2,1,0:T(8,128)(2,1)S(1)}, bf16[4,1,2,384,384]{4,3,2,1,0:T(8,128)(2,1)}, u32[]{:S(2)}) copy-start(bf16[4,1,2,384,384]{4,3,2,1,0:T(8,128)(2,1)} %param.8) | copy-start | bytes 7077892
  277.1 8.8 %all-to-all-start = ((bf16[1,2,24,4,2,384]{5,2,3,4,0,1:T(8,128)(2,1)}), bf16[1,2,24,4,2,384]{5,2,3,4,0,1:T(8,128)(2,1)S(1)}, u32[]{:S(2)}, u32[]{:S(2)}) async-start(bf16[1,2,24,4,2,384]{5,2,3,4,0,1:T(8,128)(2,1)} %copy.65), calls=%async_computation.1 | async-start | bytes 589824 | tf_op jit(solution)/shard_map/all_to_all | solution.py:132
Sparse Core Ops, SparseCore 0:
  33.5 98.3 reduce-scatter.1
  134.1 136.8 all-gather.2
